TPU v7x, 128 devices: a whole 4x4x4 slice. The times are simulated.
128 devices in a mesh: dp: 16 (over x_lo, z, core), space: 8 (over x_hi, y).
Axes of the slice: x: 4 (x_hi: 2, x_lo: 2; x = x_hi * 2 + x_lo), y: 4, z: 4, core: 2. Of those that a mesh axis runs over, the one named last changes fastest.
Arguments:
- volume: bfloat16 [16, 4, 32, 32, 128], P('dp', None, 'space'), may hold values from -6 to 6
- w_first: bfloat16 [27, 32, 4], replicated, may hold values from -0.625 to 0.625
- b_first: float32 [32], replicated, may hold values from -3 to 3
- w_second: bfloat16 [27, 64, 32], replicated, may hold values from -0.21875 to 0.21875
- b_second: float32 [64], replicated, may hold values from -3 to 3
- cotangent: bfloat16 [16, 64, 8, 256], P('dp', None, 'space'), may hold values from -0.119628906 to 0.119628906
Outputs:
- pooled_out: bfloat16 [16, 64, 8, 256], P('dp', None, 'space')
- grad_w_first: float32 [27, 32, 4], replicated
- grad_b_first: float32 [32], replicated
- grad_w_second: float32 [27, 64, 32], replicated
- grad_b_second: float32 [64], replicated
All inputs are finite; a program needn't handle non-finite values.
Results may differ from a plain program's by a relative error of at most 0.0049.
The roundings to bfloat16 on the way count: a program that leaves them out, or rounds other values in their place, can miss the bound.
Values may be sent and summed in bfloat16 or wider, within the bound.
A program may use at most 64 MiB of HBM per device.

v0:
```python
import functools

import jax
import jax.numpy as jnp
from jax import lax
from jax.experimental import pallas as pl
from jax.experimental.pallas import tpu as pltpu
from jax.sharding import PartitionSpec as P

MESH = pl.DeviceIdType.MESH
BF = jnp.bfloat16
F32 = jnp.float32

LANES = 256
COLS = 32
SLOTS = 28
TILES = 9


def dot(a, b):
    return jnp.dot(a, b, preferred_element_type=F32)


def dot_nt(a, b):
    return lax.dot_general(a, b, (((1,), (1,)), ((), ())), preferred_element_type=F32)


def lane_of(shape):
    return lax.broadcasted_iota(jnp.int32, shape, len(shape) - 1)


def shift_x(v, step):
    lane = lane_of(v.shape)
    moved = pltpu.roll(v, step % LANES, 1)
    edge = 0 if step == 1 else COLS - 1
    return jnp.where(lane % COLS == edge, 0.0, moved)


def shift_y(v, step):
    lane = lane_of(v.shape)
    moved = pltpu.roll(v, (step * COLS) % LANES, 1)
    gone = lane < COLS if step == 1 else lane >= LANES - COLS
    return jnp.where(gone, 0.0, moved)


def leaky(v):
    return jnp.where(v > 0, v, 0.3 * v)


def slope(v):
    return jnp.where(v > 0, 1.0, 0.3)


def column(row):
    n = row.shape[1]
    r = lax.broadcasted_iota(jnp.int32, (n, n), 0)
    c = lax.broadcasted_iota(jnp.int32, (n, n), 1)
    return jnp.sum(jnp.where(r == c, jnp.broadcast_to(row, (n, n)), 0.0), axis=1, keepdims=True)


def window_layer(out, layer, raw, chans, keep):
    wide = []
    for qy in range(2):
        even = raw(2 * qy).astype(F32)
        odd = raw(2 * qy + 1).astype(F32)
        if keep is not None:
            even = jnp.where(keep, even, 0.0)
            odd = jnp.where(keep, odd, 0.0)
        wide.append(jnp.concatenate([shift_x(odd, 1), even, odd, shift_x(even, -1)], axis=0))
    out[layer, 0] = shift_y(wide[1], 1).astype(BF)
    out[layer, 1] = wide[0].astype(BF)
    out[layer, 2] = wide[1].astype(BF)
    out[layer, 3] = shift_y(wide[0], -1).astype(BF)


def kernel(
    n_dp,
    n_sp,
    vol,
    w1t,
    b1,
    w2t,
    b2,
    cot,
    top_out,
    gw1_out,
    gb1_out,
    gw2_out,
    gb2_out,
    pick,
    halo_v,
    ext,
    base_w,
    w1p,
    w2p,
    w2f,
    act1,
    pooled,
    halo_p,
    win2,
    delta2,
    halo_d,
    win3,
    acc,
    g2,
    r2,
    s2,
    f2,
    g1,
    r1,
    s1,
    f1,
    halo_send,
    halo_recv,
    send_a2,
    recv_a2,
    send_b2,
    recv_b2,
    send_c2,
    recv_c2,
    send_a1,
    recv_a1,
    send_b1,
    recv_b1,
    send_c1,
    recv_c1,
):
    d = lax.axis_index("dp")
    s = lax.axis_index("space")
    left = lax.rem(s + n_sp - 1, n_sp)
    right = lax.rem(s + 1, n_sp)
    has_left = s > 0
    has_right = s < n_sp - 1

    barrier = pltpu.get_barrier_semaphore()
    for r in range(1, n_sp):
        pl.semaphore_signal(
            barrier, inc=1, device_id={"space": lax.rem(s + r, n_sp)}, device_id_type=MESH
        )
    for r in range(1, n_dp):
        pl.semaphore_signal(
            barrier, inc=1, device_id={"dp": lax.rem(d + r, n_dp)}, device_id_type=MESH
        )

    for f in range(6):
        r = lax.broadcasted_iota(jnp.int32, (128, LANES), 0)
        c = lane_of((128, LANES)) % COLS
        pick[:, f * LANES : (f + 1) * LANES] = jnp.where(r == 4 * c + f - 1, 1.0, 0.0).astype(BF)
    row = lax.broadcasted_iota(jnp.int32, (64, 512), 0)
    col = lax.broadcasted_iota(jnp.int32, (64, 512), 1)
    gather = jnp.where(
        (row // 16 == col % 4) & ((row % 16) // 4 == col // 128) & (row % 4 == (col % 128) // 32),
        1.0,
        0.0,
    ).astype(BF)
    own_y = (lax.broadcasted_iota(jnp.int32, (128, LANES), 0) % 32) // 4 == lane_of(
        (128, LANES)
    ) // COLS

    def volume_layer(layer, plane):
        parts = []
        for f in range(6):
            spread = dot(plane, pick[:, f * LANES : (f + 1) * LANES])
            parts.append(jnp.where(own_y, spread, 0.0).astype(BF))
        for qx in range(2):
            cells = dot(gather, jnp.concatenate(parts[2 * qx : 2 * qx + 4], axis=0))
            ext[qx, layer, 0] = shift_y(cells[48:64], 1).astype(BF)
            for fy in range(4):
                ext[qx, layer, fy + 1] = cells[16 * fy : 16 * fy + 16].astype(BF)
            ext[qx, layer, 5] = shift_y(cells[0:16], -1).astype(BF)

    def halo_copy(src, dst, sem, to):
        return pltpu.make_async_remote_copy(
            src_ref=src,
            dst_ref=dst,
            send_sem=halo_send.at[sem],
            recv_sem=halo_recv.at[sem],
            device_id={"space": to},
            device_id_type=MESH,
        )

    pl.semaphore_wait(barrier, n_sp - 1 + n_dp - 1)
    v_left = halo_copy(vol.at[:, 0], halo_v.at[1], 0, left)
    v_right = halo_copy(vol.at[:, 3], halo_v.at[0], 1, right)
    v_left.start()
    v_right.start()

    for z in range(4):
        volume_layer(z + 1, vol[:, z].reshape(128, 128))

    base_w[...] = jnp.zeros_like(base_w)
    for k in range(27):
        at = 4 * (16 * (k // 9) + 4 * ((k // 3) % 3) + k % 3)
        base_w[at : at + 4, 0:32] = w1t[k].astype(F32)
    base = base_w[...].T[0:32]
    for p in range(8):
        by = 4 * (16 * (p // 4) + 4 * ((p // 2) % 2) + p % 2)
        w1p[32 * p : 32 * p + 32] = (pltpu.roll(base, by, 1) if by else base).astype(BF)
    none = jnp.zeros((32, 64), F32)
    for ac in range(9):
        taps = [w2t[3 * ac + e].astype(F32) for e in range(3)]
        blocks = [
            jnp.concatenate([taps[w] if w < 3 else none, taps[w - 1] if w > 0 else none], axis=1)
            for w in range(4)
        ]
        w2p[:, 128 * ac : 128 * ac + 128] = jnp.concatenate(blocks, axis=0).T.astype(BF)
        at = 256 * (8 - ac)
        w2f[0:32, at : at + 256] = jnp.concatenate([taps[2], taps[1], taps[0], none], axis=1).astype(BF)
        w2f[32:64, at : at + 256] = jnp.concatenate([none, taps[2], taps[1], taps[0]], axis=1).astype(BF)
    b1c = column(b1[...])
    b2c = column(b2[...])

    v_left.wait()
    v_right.wait()
    for side, keep in ((0, has_left), (1, has_right)):
        plane = halo_v[side].reshape(128, 128).astype(F32)
        volume_layer(5 * side, jnp.where(keep, plane, 0.0).astype(BF))

    def first_window(q):
        qz, qy, qx = q // 4, (q // 2) % 2, q % 2
        return ext[qx, 2 * qz : 2 * qz + 4, 2 * qy : 2 * qy + 4].reshape(256, LANES)

    p_copies = []
    for qz in range(2):
        for qq in range(4):
            q = 4 * qz + qq
            act = dot(w1p[...], first_window(q)).reshape(8, 32, LANES) + b1c[None]
            act1[q] = act
            pooled[qz, qq] = (jnp.sum(leaky(act), axis=0) * 0.125).astype(BF)
        copy = halo_copy(pooled.at[qz], halo_p.at[1 - qz], 2 + qz, right if qz else left)
        copy.start()
        p_copies.append(copy)

    for qz in range(2):
        window_layer(win2, 1 + qz, lambda j, qz=qz: pooled[qz, j], 32, None)

    def second_window(pz, py, a0, a1):
        return win2[pz + a0 : pz + a1, py : py + 3].reshape((a1 - a0) * 384, LANES)

    for pz in range(2):
        for py in range(2):
            own = second_window(pz, py, 1 - pz, 3 - pz)
            acc[2 * pz + py] = dot(w2p[:, 384 * (1 - pz) : 384 * (3 - pz)], own)
    for copy in p_copies:
        copy.wait()
    grad_top = cot[...].astype(F32) * 0.125
    top = jnp.zeros((64, LANES), F32)
    d_copies = []
    for pz in range(2):
        keep = has_right if pz else has_left
        window_layer(win2, 3 * pz, lambda j, pz=pz: halo_p[pz, j], 32, keep)
        for py in range(2):
            at = 2 * pz
            act = acc[2 * pz + py] + dot(
                w2p[:, 384 * at : 384 * at + 384], second_window(pz, py, at, at + 1)
            )
            for px in range(2):
                one = act[64 * px : 64 * px + 64] + b2c
                top = top + leaky(one)
                delta2[pz, 2 * py + px] = (grad_top * slope(one)).astype(BF)
        copy = halo_copy(delta2.at[pz], halo_d.at[1 - pz], 4 + pz, right if pz else left)
        copy.start()
        d_copies.append(copy)
    top_out[...] = (top * 0.125).astype(BF)

    ones = jnp.ones((16, LANES), BF)
    grad = None
    sums = None
    for pz in range(2):
        for py in range(2):
            there = delta2[pz, 2 * py : 2 * py + 2].reshape(128, LANES)
            term = dot_nt(second_window(pz, py, 0, 3), there)
            part = dot_nt(ones, there)
            grad = term if grad is None else grad + term
            sums = part if sums is None else sums + part
    low = lane_of((16, 128)) < 64
    per2 = -(-SLOTS // n_dp)
    for k in range(27):
        at = 128 * (k // 3) + 32 * (k % 3)
        here, after = grad[at : at + 32], grad[at + 32 : at + 64]
        first = here[0:16] + pltpu.roll(after[0:16], 64, 1)
        second = pltpu.roll(here[16:32], 64, 1) + after[16:32]
        g2[k // per2, k % per2] = jnp.where(low, first, second)
    g2[27 // per2, 27 % per2] = sums + pltpu.roll(sums, 64, 1)
    for extra in range(SLOTS, per2 * (-(-SLOTS // per2))):
        g2[extra // per2, extra % per2] = jnp.zeros((16, 128), F32)

    def phase_a(src, land, send, recv, owners, start):
        for r in range(1, n_dp):
            to = lax.rem(d + r, n_dp)

            @pl.when(to < owners)
            def _():
                copy = pltpu.make_async_remote_copy(
                    src_ref=src.at[to],
                    dst_ref=land.at[d],
                    send_sem=send.at[to],
                    recv_sem=recv.at[d],
                    device_id={"dp": to},
                    device_id_type=MESH,
                )
                if start:
                    copy.start()
                else:
                    copy.wait_send()

    def wait_a(src, land, send, recv):
        for r in range(1, n_dp):
            come = lax.rem(d + r, n_dp)
            pltpu.make_async_remote_copy(
                src_ref=src.at[0],
                dst_ref=land.at[come],
                send_sem=send.at[0],
                recv_sem=recv.at[come],
                device_id={"dp": come},
                device_id_type=MESH,
            ).wait_recv()

    def phase_b(land, send, recv, start):
        for r in range(1, n_sp):
            to = lax.rem(s + r, n_sp)
            copy = pltpu.make_async_remote_copy(
                src_ref=land.at[s],
                dst_ref=land.at[s],
                send_sem=send.at[to],
                recv_sem=recv.at[s],
                device_id={"space": to},
                device_id_type=MESH,
            )
            if start:
                copy.start()
            else:
                copy.wait_send()

    def wait_b(land, send, recv):
        for r in range(1, n_sp):
            come = lax.rem(s + r, n_sp)
            pltpu.make_async_remote_copy(
                src_ref=land.at[come],
                dst_ref=land.at[come],
                send_sem=send.at[come],
                recv_sem=recv.at[come],
                device_id={"space": come},
                device_id_type=MESH,
            ).wait_recv()

    def phase_c(land, send, recv, start):
        for r in range(1, n_dp):
            to = lax.rem(d + r, n_dp)
            copy = pltpu.make_async_remote_copy(
                src_ref=land.at[d],
                dst_ref=land.at[d],
                send_sem=send.at[to],
                recv_sem=recv.at[d],
                device_id={"dp": to},
                device_id_type=MESH,
            )
            if start:
                copy.start()
            else:
                copy.wait_send()

    def wait_c(land, send, recv, owners):
        for r in range(1, n_dp):
            come = lax.rem(d + r, n_dp)

            @pl.when(come < owners)
            def _():
                pltpu.make_async_remote_copy(
                    src_ref=land.at[come],
                    dst_ref=land.at[come],
                    send_sem=send.at[come],
                    recv_sem=recv.at[come],
                    device_id={"dp": come},
                    device_id_type=MESH,
                ).wait_recv()

    own2 = -(-SLOTS // per2)
    per1 = -(-TILES // n_dp)
    own1 = -(-TILES // per1)

    phase_a(g2, r2, send_a2, recv_a2, own2, True)

    for pz in range(2):
        window_layer(win3, 1 + pz, lambda j, pz=pz: delta2[pz, j], 64, None)

    def back_window(qz, qy, a0, a1):
        return win3[qz + a0 : qz + a1, qy : qy + 3].reshape((a1 - a0) * 768, LANES)

    backs = []
    for qz in range(2):
        for qy in range(2):
            own = back_window(qz, qy, 1 - qz, 3 - qz)
            backs.append(dot(w2f[:, 768 * (1 - qz) : 768 * (3 - qz)], own))
    for copy in d_copies:
        copy.wait()
    grad1 = None
    sum1 = None
    for qz in range(2):
        keep = has_right if qz else has_left
        window_layer(win3, 3 * qz, lambda j, qz=qz: halo_d[qz, j], 64, keep)
        for qy in range(2):
            at = 2 * qz
            back = backs[2 * qz + qy] + dot(
                w2f[:, 768 * at : 768 * at + 768], back_window(qz, qy, at, at + 1)
            )
            back = back * 0.125
            for qx in range(2):
                q = 4 * qz + 2 * qy + qx
                one = back[32 * qx : 32 * qx + 32]
                delta1 = (one[None] * slope(act1[q])).astype(BF).reshape(256, LANES)
                term = dot_nt(delta1, first_window(q))
                part = dot_nt(ones[0:16], delta1)
                grad1 = term if grad1 is None else grad1 + term
                sum1 = part if sum1 is None else sum1 + part
    fold = grad1[0:32]
    for p in range(1, 8):
        by = 4 * (16 * (p // 4) + 4 * ((p // 2) % 2) + p % 2)
        fold = fold + pltpu.roll(grad1[32 * p : 32 * p + 32], LANES - by, 1)
    for t in range(8):
        rt, lt = t // 2, t % 2
        g1[t // per1, t % per1] = fold[8 * rt : 8 * rt + 8, 128 * lt : 128 * lt + 128]
    bias = sum1[0:8, 0:128] + sum1[0:8, 128:256]
    bias = bias + pltpu.roll(bias, 64, 1)
    bias = bias + pltpu.roll(bias, 96, 1)
    g1[8 // per1, 8 % per1] = bias
    for extra in range(TILES, per1 * own1):
        g1[extra // per1, extra % per1] = jnp.zeros((8, 128), F32)

    phase_a(g1, r1, send_a1, recv_a1, own1, True)

    sets = (
        (g2, r2, s2, f2, send_a2, recv_a2, send_b2, recv_b2, send_c2, recv_c2, own2),
        (g1, r1, s1, f1, send_a1, recv_a1, send_b1, recv_b1, send_c1, recv_c1, own1),
    )
    for g, r, sp, fin, sa, ra, sb, rb, sc, rc, own in sets:

        @pl.when(d < own)
        def _(g=g, r=r, sp=sp, sa=sa, ra=ra, sb=sb, rb=rb):
            r[d] = g[d]
            wait_a(g, r, sa, ra)
            total = r[0]
            for j in range(1, n_dp):
                total = total + r[j]
            sp[s] = total
            phase_b(sp, sb, rb, True)

    for g, r, sp, fin, sa, ra, sb, rb, sc, rc, own in sets:

        @pl.when(d < own)
        def _(sp=sp, fin=fin, sb=sb, rb=rb, sc=sc, rc=rc):
            wait_b(sp, sb, rb)
            total = sp[0]
            for j in range(1, n_sp):
                total = total + sp[j]
            fin[d] = total
            phase_c(fin, sc, rc, True)

    wait_c(f2, send_c2, recv_c2, own2)
    for k in range(27):
        both = f2[k // per2, k % per2]
        gw2_out[k, 0:16] = both[:, 0:64]
        gw2_out[k, 16:32] = pltpu.roll(both, 64, 1)[:, 0:64]
    gb2_out[...] = f2[27 // per2, 27 % per2][0:1, 0:64]
    wait_c(f1, send_c1, recv_c1, own1)
    rows = []
    for rt in range(4):
        rows.append(
            jnp.concatenate(
                [f1[(2 * rt + lt) // per1, (2 * rt + lt) % per1] for lt in range(2)], axis=1
            )
        )
    rows = jnp.concatenate(rows + [jnp.zeros((96, LANES), F32)], axis=0).T
    for k in range(27):
        at = 4 * (16 * (k // 9) + 4 * ((k // 3) % 3) + k % 3)
        gw1_out[k] = rows[at : at + 4, 0:32]
    gb1_out[...] = f1[8 // per1, 8 % per1][0:1, 0:32]

    for g, r, sp, fin, sa, ra, sb, rb, sc, rc, own in sets:
        phase_a(g, r, sa, ra, own, False)

        @pl.when(d < own)
        def _(sp=sp, fin=fin, sb=sb, rb=rb, sc=sc, rc=rc):
            phase_b(sp, sb, rb, False)
            phase_c(fin, sc, rc, False)


def solution(mesh):
    n_dp, n_sp = mesh.shape["dp"], mesh.shape["space"]
    per2 = -(-SLOTS // n_dp)
    per1 = -(-TILES // n_dp)
    vm = pl.BlockSpec(memory_space=pltpu.VMEM)

    def body(volume, w_first, b_first, w_second, b_second, cotangent):
        outs = pl.pallas_call(
            functools.partial(kernel, n_dp, n_sp),
            out_shape=(
                jax.ShapeDtypeStruct((64, LANES), BF),
                jax.ShapeDtypeStruct((27, 4, 32), F32),
                jax.ShapeDtypeStruct((1, 32), F32),
                jax.ShapeDtypeStruct((27, 32, 64), F32),
                jax.ShapeDtypeStruct((1, 64), F32),
            ),
            in_specs=[vm] * 6,
            out_specs=(vm,) * 5,
            scratch_shapes=[
                pltpu.VMEM((128, 6 * LANES), BF),
                pltpu.VMEM((2, 4, 32, 128), BF),
                pltpu.VMEM((2, 6, 6, 16, LANES), BF),
                pltpu.VMEM((256, 128), F32),
                pltpu.VMEM((256, 256), BF),
                pltpu.VMEM((128, 1152), BF),
                pltpu.VMEM((64, 2304), BF),
                pltpu.VMEM((8, 8, 32, LANES), F32),
                pltpu.VMEM((2, 4, 32, LANES), BF),
                pltpu.VMEM((2, 4, 32, LANES), BF),
                pltpu.VMEM((4, 4, 128, LANES), BF),
                pltpu.VMEM((2, 4, 64, LANES), BF),
                pltpu.VMEM((2, 4, 64, LANES), BF),
                pltpu.VMEM((4, 4, 256, LANES), BF),
                pltpu.VMEM((4, 128, LANES), F32),
                pltpu.VMEM((n_dp, per2, 16, 128), F32),
                pltpu.VMEM((n_dp, per2, 16, 128), F32),
                pltpu.VMEM((n_sp, per2, 16, 128), F32),
                pltpu.VMEM((n_dp, per2, 16, 128), F32),
                pltpu.VMEM((n_dp, per1, 8, 128), F32),
                pltpu.VMEM((n_dp, per1, 8, 128), F32),
                pltpu.VMEM((n_sp, per1, 8, 128), F32),
                pltpu.VMEM((n_dp, per1, 8, 128), F32),
                pltpu.SemaphoreType.DMA((6,)),
                pltpu.SemaphoreType.DMA((6,)),
            ]
            + [pltpu.SemaphoreType.DMA((n,)) for n in (n_dp, n_dp, n_sp, n_sp, n_dp, n_dp) * 2],
            compiler_params=pltpu.CompilerParams(collective_id=0, has_side_effects=True),
        )(
            volume.reshape(4, 4, 32, 128),
            w_first.transpose(0, 2, 1),
            b_first.reshape(1, 32),
            w_second.transpose(0, 2, 1),
            b_second.reshape(1, 64),
            cotangent.reshape(64, LANES),
        )
        top, gw1, gb1, gw2, gb2 = outs
        return (
            top.reshape(1, 64, 1, LANES),
            gw1.transpose(0, 2, 1),
            gb1.reshape(32),
            gw2.transpose(0, 2, 1),
            gb2.reshape(64),
        )

    in_specs = (
        P("dp", None, "space", None, None),
        P(),
        P(),
        P(),
        P(),
        P("dp", None, "space", None),
    )
    out_specs = (P("dp", None, "space", None), P(), P(), P(), P())
    return jax.shard_map(body, mesh=mesh, in_specs=in_specs, out_specs=out_specs, check_vma=False)
```

profile of v0, /device:TPU:1, one launch (start us, length us, event | category | flops | bytes accessed | tf_op | source)
XLA Modules:
  0.0 49.9 jit_solution(3174177950296130280)
XLA Ops:
  0.6 44.4 %shard_map.101 = (bf16[64,256]{1,0:T(8,128)(2,1)}, f32[27,4,32]{2,1,0:T(4,128)}, f32[1,32]{1,0:T(1,128)}, f32[27,32,64]{2,1,0:T(8,128)}, f32[1,64]{1,0:T(1,128)}) custom-call(bf16[4,4,32,128]{3,2,1,0:T(8,128)(2,1)} %bitcast.13, bf16[27,4,32]{2,1,0:T(4,128)(2,1)} %bitcast.17, f32[1,32]{1,0:T(1,128)} %bitcast.18, bf16[27,32,64]{2,1,0:T(8,128)(2,1)} %bitcast.12, ...), custom_call_target="tpu_custom_call" | custom-call | tf_op jit(solution)/shard_map/pallas_call | solution.py:495
  45.0 0.0 copy-start
  45.0 1.4 %copy.16 = bf16[1,64,1,256]{3,1,2,0:T(8,128)(2,1)} copy(bf16[1,64,1,256]{3,1,2,0:T(8,128)(2,1)} %bitcast.16) | data formatting | bytes 65536
  46.4 0.0 copy-done
  46.4 0.0 copy-start.2
  46.4 0.6 %copy.17 = f32[27,32,4]{1,2,0:T(4,128)} copy(f32[27,32,4]{1,2,0:T(4,128)S(1)} %bitcast.14) | data formatting | bytes 27648
  47.0 0.0 copy-done.2
  47.1 0.5 %copy.18 = f32[32]{0:T(128)} copy(f32[32]{0:T(128)S(1)} %bitcast.21) | data formatting | bytes 256
  47.6 0.0 copy-start.1
  47.6 1.8 %copy.19 = f32[27,64,32]{1,2,0:T(8,128)} copy(f32[27,64,32]{1,2,0:T(8,128)} %bitcast.11) | data formatting | bytes 442368
  49.4 0.0 copy-done.1
  49.4 0.5 %copy.20 = f32[64]{0:T(128)} copy(f32[64]{0:T(128)S(1)} %bitcast.20) | data formatting | bytes 512
Async XLA Ops:
  45.0 1.4 %copy-start = (f32[27,4,32]{2,1,0:T(4,128)S(1)}, f32[27,4,32]{2,1,0:T(4,128)}, u32[]{:S(2)}) copy-start(f32[27,4,32]{2,1,0:T(4,128)} %get-tuple-element.11) | copy-start | bytes 41476
  46.4 0.7 %copy-start.2 = (f32[1,32]{1,0:T(1,128)S(1)}, f32[1,32]{1,0:T(1,128)}, u32[]{:S(2)}) copy-start(f32[1,32]{1,0:T(1,128)} %get-tuple-element.12) | copy-start | bytes 388
  47.6 1.8 %copy-start.1 = (f32[1,64]{1,0:T(1,128)S(1)}, f32[1,64]{1,0:T(1,128)}, u32[]{:S(2)}) copy-start(f32[1,64]{1,0:T(1,128)} %get-tuple-element.14) | copy-start | bytes 772
where the time goes:
time: 50.1 us; the launch traced here: 49.9 us
  Pallas kernels  44.4 us (89%)
  local copies, waits for them, and re-layouts  4.89 us (10%)
  between operations  0.65 us (1%)
    pallas_call x1, Pallas kernels, body(): pl.pallas_call(functools.partial(kernel, n_dp, n_sp), out_shape=(jax.Shap...  44.4 us
    unnamed x11, local copies, waits for them, and re-layouts  4.89 us

commit v1 on v0

v1 whole, which is shorter than its diff:
```python
import functools

import jax
import jax.numpy as jnp
from jax import lax
from jax.experimental import pallas as pl
from jax.experimental.pallas import tpu as pltpu
from jax.sharding import PartitionSpec as P

MESH = pl.DeviceIdType.MESH
BF = jnp.bfloat16
F32 = jnp.float32

LANES = 256
COLS = 32
SLOTS = 28
TILES = 8


def dot(a, b):
    return jnp.dot(a, b, preferred_element_type=F32)


def dot_nt(a, b):
    return lax.dot_general(a, b, (((1,), (1,)), ((), ())), preferred_element_type=F32)


def lane_of(shape):
    return lax.broadcasted_iota(jnp.int32, shape, len(shape) - 1)


def shift_x(v, step):
    lane = lane_of(v.shape)
    moved = pltpu.roll(v, step % LANES, 1)
    edge = 0 if step == 1 else COLS - 1
    return jnp.where(lane % COLS == edge, 0.0, moved)


def shift_y(v, step):
    lane = lane_of(v.shape)
    moved = pltpu.roll(v, (step * COLS) % LANES, 1)
    gone = lane < COLS if step == 1 else lane >= LANES - COLS
    return jnp.where(gone, 0.0, moved)


def leaky(v):
    return jnp.where(v > 0, v, 0.3 * v)


def slope(v):
    return jnp.where(v > 0, 1.0, 0.3)


def column(row):
    n = row.shape[1]
    r = lax.broadcasted_iota(jnp.int32, (n, n), 0)
    c = lax.broadcasted_iota(jnp.int32, (n, n), 1)
    return jnp.sum(jnp.where(r == c, jnp.broadcast_to(row, (n, n)), 0.0), axis=1, keepdims=True)


def window_layer(out, layer, raw, chans, keep):
    wide = []
    for qy in range(2):
        even = raw(2 * qy).astype(F32)
        odd = raw(2 * qy + 1).astype(F32)
        if keep is not None:
            even = jnp.where(keep, even, 0.0)
            odd = jnp.where(keep, odd, 0.0)
        wide.append(jnp.concatenate([shift_x(odd, 1), even, odd, shift_x(even, -1)], axis=0))
    out[layer, 0] = shift_y(wide[1], 1).astype(BF)
    out[layer, 1] = wide[0].astype(BF)
    out[layer, 2] = wide[1].astype(BF)
    out[layer, 3] = shift_y(wide[0], -1).astype(BF)


def kernel(
    n_dp,
    n_sp,
    vol_h,
    w1_h,
    b1_h,
    w2_h,
    b2_h,
    cot_h,
    top_out,
    f1,
    f2,
    vol,
    w1t,
    b1,
    w2t,
    b2,
    cot,
    pick,
    halo_v,
    ext,
    base_w,
    w1p,
    w2p,
    w2f,
    act1,
    pooled,
    halo_p,
    win2,
    delta2,
    give,
    halo_d,
    win3,
    acc,
    g2,
    r2,
    s2,
    t2,
    g1,
    r1,
    s1,
    t1,
    local_sem,
    halo_send,
    halo_recv,
    send_a2,
    recv_a2,
    send_b2,
    recv_b2,
    send_c2,
    recv_c2,
    send_a1,
    recv_a1,
    send_b1,
    recv_b1,
    send_c1,
    recv_c1,
):
    d = lax.axis_index("dp")
    s = lax.axis_index("space")
    left = lax.rem(s + n_sp - 1, n_sp)
    right = lax.rem(s + 1, n_sp)
    has_left = s > 0
    has_right = s < n_sp - 1

    n_g = n_dp // 2
    n_h = 2 * n_sp
    half, g = d // n_g, lax.rem(d, n_g)
    h = half * n_sp + s

    barrier = pltpu.get_barrier_semaphore()
    for r in range(1, n_sp):
        pl.semaphore_signal(
            barrier, inc=1, device_id={"space": lax.rem(s + r, n_sp)}, device_id_type=MESH
        )
    for r in range(1, n_dp):
        pl.semaphore_signal(
            barrier, inc=1, device_id={"dp": lax.rem(d + r, n_dp)}, device_id_type=MESH
        )
    for r in range(1, n_sp):
        pl.semaphore_signal(
            barrier,
            inc=1,
            device_id={"dp": (1 - half) * n_g + g, "space": lax.rem(s + r, n_sp)},
            device_id_type=MESH,
        )
    loads = [
        pltpu.make_async_copy(src, dst, local_sem.at[n])
        for n, (src, dst) in enumerate(
            ((vol_h, vol), (w1_h, w1t), (w2_h, w2t), (b1_h, b1), (b2_h, b2), (cot_h, cot))
        )
    ]
    for copy in loads:
        copy.start()

    for f in range(6):
        r = lax.broadcasted_iota(jnp.int32, (128, LANES), 0)
        c = lane_of((128, LANES)) % COLS
        pick[:, f * LANES : (f + 1) * LANES] = jnp.where(r == 4 * c + f - 1, 1.0, 0.0).astype(BF)
    row = lax.broadcasted_iota(jnp.int32, (64, 512), 0)
    col = lax.broadcasted_iota(jnp.int32, (64, 512), 1)
    gather = jnp.where(
        (row // 16 == col % 4) & ((row % 16) // 4 == col // 128) & (row % 4 == (col % 128) // 32),
        1.0,
        0.0,
    ).astype(BF)
    own_y = (lax.broadcasted_iota(jnp.int32, (128, LANES), 0) % 32) // 4 == lane_of(
        (128, LANES)
    ) // COLS

    def volume_layer(layer, plane):
        parts = []
        for f in range(6):
            spread = dot(plane, pick[:, f * LANES : (f + 1) * LANES])
            parts.append(jnp.where(own_y, spread, 0.0).astype(BF))
        for qx in range(2):
            cells = dot(gather, jnp.concatenate(parts[2 * qx : 2 * qx + 4], axis=0))
            ext[qx, layer, 0] = shift_y(cells[48:64], 1).astype(BF)
            for fy in range(4):
                ext[qx, layer, fy + 1] = cells[16 * fy : 16 * fy + 16].astype(BF)
            ext[qx, layer, 5] = shift_y(cells[0:16], -1).astype(BF)

    def halo_copy(src, dst, sem, to):
        return pltpu.make_async_remote_copy(
            src_ref=src,
            dst_ref=dst,
            send_sem=halo_send.at[sem],
            recv_sem=halo_recv.at[sem],
            device_id={"space": to},
            device_id_type=MESH,
        )

    loads[0].wait()
    pl.semaphore_wait(barrier, 2 * (n_sp - 1) + n_dp - 1)
    v_left = halo_copy(vol.at[:, 0], halo_v.at[1], 0, left)
    v_right = halo_copy(vol.at[:, 3], halo_v.at[0], 1, right)
    v_left.start()
    v_right.start()

    for z in range(4):
        volume_layer(z + 1, vol[:, z].reshape(128, 128))

    for copy in loads[1:]:
        copy.wait()
    base_w[...] = jnp.zeros_like(base_w)
    for k in range(27):
        at = 4 * (16 * (k // 9) + 4 * ((k // 3) % 3) + k % 3)
        base_w[at : at + 4, 0:32] = w1t[k].astype(F32)
    base = base_w[...].T[0:32]
    for p in range(8):
        by = 4 * (16 * (p // 4) + 4 * ((p // 2) % 2) + p % 2)
        w1p[32 * p : 32 * p + 32] = (pltpu.roll(base, by, 1) if by else base).astype(BF)
    none = jnp.zeros((32, 64), F32)
    for ac in range(9):
        taps = [w2t[3 * ac + e].astype(F32) for e in range(3)]
        blocks = [
            jnp.concatenate([taps[w] if w < 3 else none, taps[w - 1] if w > 0 else none], axis=1)
            for w in range(4)
        ]
        w2p[:, 128 * ac : 128 * ac + 128] = jnp.concatenate(blocks, axis=0).T.astype(BF)
        down, at = 64 * (2 - ac // 3), 256 * (2 - ac % 3)
        w2f[down : down + 32, at : at + 256] = jnp.concatenate(
            [taps[2], taps[1], taps[0], none], axis=1
        ).astype(BF)
        w2f[down + 32 : down + 64, at : at + 256] = jnp.concatenate(
            [none, taps[2], taps[1], taps[0]], axis=1
        ).astype(BF)
    b1c = column(b1[...])
    b2c = column(b2[...])

    v_left.wait_recv()
    v_right.wait_recv()
    for side, keep in ((0, has_left), (1, has_right)):
        plane = halo_v[side].reshape(128, 128).astype(F32)
        volume_layer(5 * side, jnp.where(keep, plane, 0.0).astype(BF))

    def first_window(q):
        qz, qy, qx = q // 4, (q // 2) % 2, q % 2
        return ext[qx, 2 * qz : 2 * qz + 4, 2 * qy : 2 * qy + 4].reshape(256, LANES)

    p_copies = []
    for qz in range(2):
        for qq in range(4):
            q = 4 * qz + qq
            act = dot(w1p[...], first_window(q)).reshape(8, 32, LANES) + b1c[None]
            act1[q] = act
            pooled[qz, qq] = (jnp.sum(leaky(act), axis=0) * 0.125).astype(BF)
        copy = halo_copy(pooled.at[qz], halo_p.at[1 - qz], 2 + qz, right if qz else left)
        copy.start()
        p_copies.append(copy)

    for qz in range(2):
        window_layer(win2, 1 + qz, lambda j, qz=qz: pooled[qz, j], 32, None)

    def second_window(pz, py, a0, a1):
        return win2[pz + a0 : pz + a1, py : py + 3].reshape((a1 - a0) * 384, LANES)

    for pz in range(2):
        for py in range(2):
            own = second_window(pz, py, 1 - pz, 3 - pz)
            acc[2 * pz + py] = dot(w2p[:, 384 * (1 - pz) : 384 * (3 - pz)], own)
    grad_top = cot[...].astype(F32) * 0.125
    top = jnp.zeros((64, LANES), F32)
    backs = [[None, None], [None, None]]
    d_copies = []
    for pz in range(2):
        p_copies[1 - pz].wait_recv()
        keep = has_right if pz else has_left
        window_layer(win2, 3 * pz, lambda j, pz=pz: halo_p[pz, j], 32, keep)
        for py in range(2):
            at = 2 * pz
            act = acc[2 * pz + py] + dot(
                w2p[:, 384 * at : 384 * at + 384], second_window(pz, py, at, at + 1)
            )
            for px in range(2):
                one = act[64 * px : 64 * px + 64] + b2c
                top = top + leaky(one)
                delta2[pz, 2 * py + px] = (grad_top * slope(one)).astype(BF)
        window_layer(win3, pz, lambda j, pz=pz: delta2[pz, j], 64, None)
        for qy in range(2):
            three = dot(w2f[...], win3[pz, qy : qy + 3].reshape(768, LANES))
            for a in range(3):
                qz, part = 1 + pz - a, three[64 * a : 64 * a + 64]
                if 0 <= qz < 2:
                    there = backs[qz][qy]
                    backs[qz][qy] = part if there is None else there + part
                else:
                    give[pz, qy] = part.astype(BF)
        copy = halo_copy(give.at[pz], halo_d.at[1 - pz], 4 + pz, right if pz else left)
        copy.start()
        d_copies.append(copy)
    top_out[...] = (top * 0.125).astype(BF)

    ones = jnp.ones((16, LANES), BF)
    grad = None
    sums = None
    for pz in range(2):
        for py in range(2):
            there = delta2[pz, 2 * py : 2 * py + 2].reshape(128, LANES)
            term = dot_nt(second_window(pz, py, 0, 3), there)
            part = dot_nt(ones, there)
            grad = term if grad is None else grad + term
            sums = part if sums is None else sums + part
    low = lane_of((16, 128)) < 64
    per2 = -(-SLOTS // n_dp)
    for k in range(27):
        at = 128 * (k // 3) + 32 * (k % 3)
        here, after = grad[at : at + 32], grad[at + 32 : at + 64]
        first = here[0:16] + pltpu.roll(after[0:16], 64, 1)
        second = pltpu.roll(here[16:32], 64, 1) + after[16:32]
        g2[k // per2, k % per2] = jnp.where(low, first, second)
    g2[27 // per2, 27 % per2] = sums + pltpu.roll(sums, 64, 1)
    for extra in range(SLOTS, per2 * (-(-SLOTS // per2))):
        g2[extra // per2, extra % per2] = jnp.zeros((16, 128), F32)

    def to_dp(j):
        return {"dp": j}

    def to_space(j):
        return {"space": j}

    def to_g(j):
        return {"dp": half * n_g + j}

    def to_h(j):
        return {"dp": (j // n_sp) * n_g + g, "space": lax.rem(j, n_sp)}

    def send_all(me, n, owners, where, src, dst, send, recv, start):
        for r in range(1, n):
            to = lax.rem(me + r, n)

            def one():
                copy = pltpu.make_async_remote_copy(
                    src_ref=src(to),
                    dst_ref=dst,
                    send_sem=send.at[to],
                    recv_sem=recv.at[me],
                    device_id=where(to),
                    device_id_type=MESH,
                )
                if start:
                    copy.start()
                else:
                    copy.wait_send()

            if owners < n:
                pl.when(to < owners)(one)
            else:
                one()

    def take_all(me, n, owners, where, land, send, recv):
        for r in range(1, n):
            come = lax.rem(me + r, n)

            def one():
                pltpu.make_async_remote_copy(
                    src_ref=land.at[come],
                    dst_ref=land.at[come],
                    send_sem=send.at[come],
                    recv_sem=recv.at[come],
                    device_id=where(come),
                    device_id_type=MESH,
                ).wait_recv()

            if owners < n:
                pl.when(come < owners)(one)
            else:
                one()

    own2 = -(-SLOTS // per2)
    per1 = TILES // n_g

    def start_a2(start):
        send_all(d, n_dp, own2, to_dp, lambda to: g2.at[to], r2.at[d], send_a2, recv_a2, start)

    def start_b2(start):
        send_all(s, n_sp, n_sp, to_space, lambda to: s2.at[s], s2.at[s], send_b2, recv_b2, start)

    def start_c2(start):
        send_all(d, n_dp, n_dp, to_dp, lambda to: t2, f2.at[d], send_c2, recv_c2, start)

    def start_a1(start):
        send_all(g, n_g, n_g, to_g, lambda to: g1.at[to], r1.at[g], send_a1, recv_a1, start)

    def start_b1(start):
        send_all(h, n_h, n_h, to_h, lambda to: s1.at[h], s1.at[h], send_b1, recv_b1, start)

    def start_c1(start):
        send_all(g, n_g, n_g, to_g, lambda to: t1, f1.at[g], send_c1, recv_c1, start)

    def added(ref, n):
        total = ref[0]
        for j in range(1, n):
            total = total + ref[j]
        return total

    start_a2(True)

    grad1 = None
    sum1 = None
    for qz in range(2):
        keep = has_right if qz else has_left
        d_copies[1 - qz].wait_recv()
        for qy in range(2):
            back = backs[qz][qy] + jnp.where(keep, halo_d[qz, qy].astype(F32), 0.0)
            back = back * 0.125
            for qx in range(2):
                q = 4 * qz + 2 * qy + qx
                one = back[32 * qx : 32 * qx + 32]
                delta1 = (one[None] * slope(act1[q])).astype(BF).reshape(256, LANES)
                term = dot_nt(delta1, first_window(q))
                part = dot_nt(ones[0:16], delta1)
                grad1 = term if grad1 is None else grad1 + term
                sum1 = part if sum1 is None else sum1 + part
    fold = grad1[0:32]
    for p in range(1, 8):
        by = 4 * (16 * (p // 4) + 4 * ((p // 2) % 2) + p % 2)
        fold = fold + pltpu.roll(grad1[32 * p : 32 * p + 32], LANES - by, 1)
    bias = sum1[0:8, 0:128] + sum1[0:8, 128:256]
    bias = bias + pltpu.roll(bias, 64, 1)
    bias = bias + pltpu.roll(bias, 96, 1)
    fold = jnp.where(lane_of((32, LANES)) == LANES - 1, column(bias[0:1, 0:32]), fold)
    for t in range(8):
        rt, lt = t // 2, t % 2
        g1[t // per1, t % per1] = fold[8 * rt : 8 * rt + 8, 128 * lt : 128 * lt + 128]

    start_a1(True)

    @pl.when(d < own2)
    def _():
        r2[d] = g2[d]
        take_all(d, n_dp, n_dp, to_dp, r2, send_a2, recv_a2)
        s2[s] = added(r2, n_dp)
        start_b2(True)

    r1[g] = g1[g]
    take_all(g, n_g, n_g, to_g, r1, send_a1, recv_a1)
    s1[h] = added(r1, n_g)
    start_b1(True)

    mine2 = pltpu.make_async_copy(t2, f2.at[d], local_sem.at[0])
    mine1 = pltpu.make_async_copy(t1, f1.at[g], local_sem.at[1])

    @pl.when(d < own2)
    def _():
        take_all(s, n_sp, n_sp, to_space, s2, send_b2, recv_b2)
        t2[...] = added(s2, n_sp).astype(BF)
        start_c2(True)
        mine2.start()

    take_all(h, n_h, n_h, to_h, s1, send_b1, recv_b1)
    t1[...] = added(s1, n_h)
    start_c1(True)
    mine1.start()

    for copy in [v_left, v_right] + p_copies + d_copies:
        copy.wait_send()
    start_a2(False)
    start_a1(False)
    start_b1(False)

    @pl.when(d < own2)
    def _():
        start_b2(False)
        mine2.wait()
        start_c2(False)

    mine1.wait()
    start_c1(False)
    take_all(d, n_dp, own2, to_dp, f2, send_c2, recv_c2)
    take_all(g, n_g, n_g, to_g, f1, send_c1, recv_c1)


def finish(per2, per1, top, f1, f2, top_out, gw1_out, gb1_out, gw2_out, gb2_out):
    top_out[...] = top[...]
    for k in range(27):
        both = f2[k // per2, k % per2].astype(F32)
        gw2_out[k, 0:16] = both[:, 0:64]
        gw2_out[k, 16:32] = pltpu.roll(both, 64, 1)[:, 0:64]
    gb2_out[...] = f2[27 // per2, 27 % per2].astype(F32)[0:1, 0:64]
    rows = []
    for rt in range(4):
        tiles = [f1[(2 * rt + lt) // per1, (2 * rt + lt) % per1] for lt in range(2)]
        rows.append(jnp.concatenate(tiles, axis=1))
    rows = jnp.concatenate(rows + [jnp.zeros((96, LANES), F32)], axis=0).T
    for k in range(27):
        at = 4 * (16 * (k // 9) + 4 * ((k // 3) % 3) + k % 3)
        gw1_out[k] = rows[at : at + 4, 0:32]
    gb1_out[...] = rows[LANES - 1 : LANES, 0:32]


def solution(mesh):
    n_dp, n_sp = mesh.shape["dp"], mesh.shape["space"]
    per2 = -(-SLOTS // n_dp)
    own2 = -(-SLOTS // per2)
    n_g, n_h = n_dp // 2, 2 * n_sp
    per1 = TILES // n_g
    vm = pl.BlockSpec(memory_space=pltpu.VMEM)
    anywhere = pl.BlockSpec(memory_space=pl.ANY)

    def body(volume, w_first, b_first, w_second, b_second, cotangent):
        parts = pl.pallas_call(
            functools.partial(kernel, n_dp, n_sp),
            out_shape=(
                jax.ShapeDtypeStruct((64, LANES), BF),
                jax.ShapeDtypeStruct((n_g, per1, 8, 128), F32),
                jax.ShapeDtypeStruct((own2, per2, 16, 128), BF),
            ),
            in_specs=[anywhere] * 6,
            out_specs=(vm, anywhere, anywhere),
            scratch_shapes=[
                pltpu.VMEM((4, 4, 32, 128), BF),
                pltpu.VMEM((27, 4, 32), BF),
                pltpu.VMEM((1, 32), F32),
                pltpu.VMEM((27, 32, 64), BF),
                pltpu.VMEM((1, 64), F32),
                pltpu.VMEM((64, LANES), BF),
                pltpu.VMEM((128, 6 * LANES), BF),
                pltpu.VMEM((2, 4, 32, 128), BF),
                pltpu.VMEM((2, 6, 6, 16, LANES), BF),
                pltpu.VMEM((256, 128), F32),
                pltpu.VMEM((256, 256), BF),
                pltpu.VMEM((128, 1152), BF),
                pltpu.VMEM((192, 768), BF),
                pltpu.VMEM((8, 8, 32, LANES), F32),
                pltpu.VMEM((2, 4, 32, LANES), BF),
                pltpu.VMEM((2, 4, 32, LANES), BF),
                pltpu.VMEM((4, 4, 128, LANES), BF),
                pltpu.VMEM((2, 4, 64, LANES), BF),
                pltpu.VMEM((2, 2, 64, LANES), BF),
                pltpu.VMEM((2, 2, 64, LANES), BF),
                pltpu.VMEM((2, 4, 256, LANES), BF),
                pltpu.VMEM((4, 128, LANES), F32),
                pltpu.VMEM((n_dp, per2, 16, 128), F32),
                pltpu.VMEM((n_dp, per2, 16, 128), F32),
                pltpu.VMEM((n_sp, per2, 16, 128), F32),
                pltpu.VMEM((per2, 16, 128), BF),
                pltpu.VMEM((n_g, per1, 8, 128), F32),
                pltpu.VMEM((n_g, per1, 8, 128), F32),
                pltpu.VMEM((n_h, per1, 8, 128), F32),
                pltpu.VMEM((per1, 8, 128), F32),
            ]
            + [
                pltpu.SemaphoreType.DMA((n,))
                for n in (6, 6, 6)
                + (n_dp, n_dp, n_sp, n_sp, n_dp, n_dp)
                + (n_g, n_g, n_h, n_h, n_g, n_g)
            ],
            compiler_params=pltpu.CompilerParams(collective_id=0, has_side_effects=True),
            name="step",
        )(
            volume.reshape(4, 4, 32, 128),
            w_first.transpose(0, 2, 1),
            b_first.reshape(1, 32),
            w_second.transpose(0, 2, 1),
            b_second.reshape(1, 64),
            cotangent.reshape(64, LANES),
        )
        top, gw1, gb1, gw2, gb2 = pl.pallas_call(
            functools.partial(finish, per2, per1),
            out_shape=(
                jax.ShapeDtypeStruct((64, LANES), BF),
                jax.ShapeDtypeStruct((27, 4, 32), F32),
                jax.ShapeDtypeStruct((1, 32), F32),
                jax.ShapeDtypeStruct((27, 32, 64), F32),
                jax.ShapeDtypeStruct((1, 64), F32),
            ),
            in_specs=[vm] * 3,
            out_specs=(vm,) * 5,
            name="finish",
        )(*parts)
        return (
            top.reshape(1, 64, 1, LANES),
            gw1.transpose(0, 2, 1),
            gb1.reshape(32),
            gw2.transpose(0, 2, 1),
            gb2.reshape(64),
        )

    in_specs = (
        P("dp", None, "space", None, None),
        P(),
        P(),
        P(),
        P(),
        P("dp", None, "space", None),
    )
    out_specs = (P("dp", None, "space", None), P(), P(), P(), P())
    return jax.shard_map(body, mesh=mesh, in_specs=in_specs, out_specs=out_specs, check_vma=False)
```

time: 50.1 us -> 43.1 us (0.86)
  local copies, waits for them, and re-layouts: 4.89 us -> 0 us
  Pallas kernels: 44.4 us -> 42.4 us
    unnamed x11 -> x0, local copies, waits for them, and re-layouts: 4.89 us -> none
    pallas_call x1, Pallas kernels: 44.4 us -> 40.5 us  [body(): pl.pallas_call(functools.partial(kernel, n_dp, n_sp), out_shape=(jax.Shap...]
    pallas_call x0 -> x1, Pallas kernels: none -> 1.81 us  [body(): pl.pallas_call(functools.partial(finish, per2, per1), out_shape=(jax.Shap...]
where the time goes in v1:
time: 43.1 us; the launch traced here: 43 us
  Pallas kernels  42.4 us (98%)
  between operations  0.64 us (1%)
    pallas_call x1, Pallas kernels, body(): pl.pallas_call(functools.partial(kernel, n_dp, n_sp), out_shape=(jax.Shap...  40.5 us
    pallas_call x1, Pallas kernels, body(): pl.pallas_call(functools.partial(finish, per2, per1), out_shape=(jax.Shap...  1.81 us

profile of v1, /device:TPU:1, one launch (start us, length us, event | category | flops | bytes accessed | tf_op | source)
XLA Modules:
  0.0 43.0 jit_solution(12408247743861765127)
XLA Ops:
  0.6 40.5 %step.1 = (bf16[64,256]{1,0:T(8,128)(2,1)}, f32[8,1,8,128]{3,2,1,0:T(8,128)}, bf16[14,2,16,128]{3,2,1,0:T(8,128)(2,1)}) custom-call(bf16[4,4,32,128]{3,2,1,0:T(8,128)(2,1)} %bitcast.12, bf16[27,4,32]{2,1,0:T(4,128)(2,1)} %bitcast.14, f32[1,32]{1,0:T(1,128)} %bitcast.15, bf16[27,32,64]{2,1,0:T(8,128)(2,1)} %bitcast.11, f32[1,64]{1,0:T(1,128)} %bitcast.16, ...), custom_call_target="tpu_custom_call" | custom-call | tf_op jit(solution)/shard_map/step/pallas_call | solution.py:517
  41.2 1.8 %finish.1 = (bf16[64,256]{1,0:T(8,128)(2,1)}, f32[27,4,32]{2,1,0:T(4,128)}, f32[1,32]{1,0:T(1,128)}, f32[27,32,64]{2,1,0:T(8,128)}, f32[1,64]{1,0:T(1,128)}) custom-call(bf16[64,256]{1,0:T(8,128)(2,1)} %get-tuple-element.13.top, f32[8,1,8,128]{3,2,1,0:T(8,128)} %get-tuple-element.14.f1, bf16[14,2,16,128]{3,2,1,0:T(8,128)(2,1)} %get-tuple-element.15.f2), custom_call_target="tpu_custom_call" | custom-call | tf_op jit(solution)/shard_map/finish/pallas_call | solution.py:574

commit v2 on v1

--- a/solution.py
+++ b/solution.py
@@ -44,7 +44,7 @@
 
 
 def leaky(v):
-    return jnp.where(v > 0, v, 0.3 * v)
+    return jnp.maximum(v, 0.3 * v)
 
 
 def slope(v):
@@ -107,6 +107,7 @@
     halo_d,
     win3,
     acc,
+    d1,
     g2,
     r2,
     s2,
@@ -116,20 +117,8 @@
     s1,
     t1,
     local_sem,
-    halo_send,
-    halo_recv,
-    send_a2,
-    recv_a2,
-    send_b2,
-    recv_b2,
-    send_c2,
-    recv_c2,
-    send_a1,
-    recv_a1,
-    send_b1,
-    recv_b1,
-    send_c1,
-    recv_c1,
+    send_sem,
+    recv_sem,
 ):
     d = lax.axis_index("dp")
     s = lax.axis_index("space")
@@ -140,25 +129,52 @@
 
     n_g = n_dp // 2
     n_h = 2 * n_sp
+    n_z, n_y = n_g // 2, n_sp // 2
     half, g = d // n_g, lax.rem(d, n_g)
+    z, core = g // 2, lax.rem(g, 2)
+    x_hi, y = s // n_y, lax.rem(s, n_y)
     h = half * n_sp + s
 
+    def ring(step, n):
+        return min(step, n - step)
+
+    def peers(x_lo_too, z_too, space_too):
+        found = []
+        for dx in range(2 if x_lo_too else 1):
+            for dz in range(n_z if z_too else 1):
+                for dc in range(2 if z_too else 1):
+                    for dh in range(2 if space_too else 1):
+                        for dy in range(n_y if space_too else 1):
+                            if dx + dz + dc + dh + dy == 0:
+                                continue
+                            hops = ring(dz, n_z) + ring(dy, n_y) + (1 if dx else 2 * dh)
+                            found.append((hops, dx, dz, dc, dh, dy))
+        found.sort(reverse=True)
+        out = []
+        for _, dx, dz, dc, dh, dy in found:
+            half_to = lax.rem(half + dx, 2)
+            g_to = lax.rem(z + dz, n_z) * 2 + lax.rem(core + dc, 2)
+            s_to = lax.rem(x_hi + dh, 2) * n_y + lax.rem(y + dy, n_y)
+            if space_too:
+                at = half_to * n_sp + s_to if x_lo_too else s_to
+            else:
+                at = half_to * n_g + g_to if x_lo_too else g_to
+            device = {}
+            if x_lo_too or z_too:
+                device["dp"] = half_to * n_g + g_to
+            if space_too:
+                device["space"] = s_to
+            out.append((at, device))
+        return out
+
+    dp_peers = peers(True, True, False)
+    g_peers = peers(False, True, False)
+    h_peers = peers(True, False, True)
+    s_peers = peers(False, False, True)
+
     barrier = pltpu.get_barrier_semaphore()
-    for r in range(1, n_sp):
-        pl.semaphore_signal(
-            barrier, inc=1, device_id={"space": lax.rem(s + r, n_sp)}, device_id_type=MESH
-        )
-    for r in range(1, n_dp):
-        pl.semaphore_signal(
-            barrier, inc=1, device_id={"dp": lax.rem(d + r, n_dp)}, device_id_type=MESH
-        )
-    for r in range(1, n_sp):
-        pl.semaphore_signal(
-            barrier,
-            inc=1,
-            device_id={"dp": (1 - half) * n_g + g, "space": lax.rem(s + r, n_sp)},
-            device_id_type=MESH,
-        )
+    for _, device in h_peers + dp_peers:
+        pl.semaphore_signal(barrier, inc=1, device_id=device, device_id_type=MESH)
     loads = [
         pltpu.make_async_copy(src, dst, local_sem.at[n])
         for n, (src, dst) in enumerate(
@@ -179,41 +195,46 @@
         1.0,
         0.0,
     ).astype(BF)
-    own_y = (lax.broadcasted_iota(jnp.int32, (128, LANES), 0) % 32) // 4 == lane_of(
-        (128, LANES)
+    own_y = (lax.broadcasted_iota(jnp.int32, (256, LANES), 0) % 32) // 4 == lane_of(
+        (256, LANES)
     ) // COLS
 
-    def volume_layer(layer, plane):
+    def volume_layers(layers, planes):
+        both = jnp.concatenate(planes, axis=0)
         parts = []
         for f in range(6):
-            spread = dot(plane, pick[:, f * LANES : (f + 1) * LANES])
+            spread = dot(both, pick[:, f * LANES : (f + 1) * LANES])
             parts.append(jnp.where(own_y, spread, 0.0).astype(BF))
-        for qx in range(2):
-            cells = dot(gather, jnp.concatenate(parts[2 * qx : 2 * qx + 4], axis=0))
-            ext[qx, layer, 0] = shift_y(cells[48:64], 1).astype(BF)
-            for fy in range(4):
-                ext[qx, layer, fy + 1] = cells[16 * fy : 16 * fy + 16].astype(BF)
-            ext[qx, layer, 5] = shift_y(cells[0:16], -1).astype(BF)
+        for n, layer in enumerate(layers):
+            for qx in range(2):
+                mine = [part[128 * n : 128 * n + 128] for part in parts[2 * qx : 2 * qx + 4]]
+                cells = dot(gather, jnp.concatenate(mine, axis=0))
+                ext[qx, layer, 0] = shift_y(cells[48:64], 1).astype(BF)
+                for fy in range(4):
+                    ext[qx, layer, fy + 1] = cells[16 * fy : 16 * fy + 16].astype(BF)
+                ext[qx, layer, 5] = shift_y(cells[0:16], -1).astype(BF)
 
     def halo_copy(src, dst, sem, to):
         return pltpu.make_async_remote_copy(
             src_ref=src,
             dst_ref=dst,
-            send_sem=halo_send.at[sem],
-            recv_sem=halo_recv.at[sem],
+            send_sem=send_sem.at[sem],
+            recv_sem=recv_sem.at[sem],
             device_id={"space": to},
             device_id_type=MESH,
         )
 
     loads[0].wait()
-    pl.semaphore_wait(barrier, 2 * (n_sp - 1) + n_dp - 1)
+    pl.semaphore_wait(barrier, n_h - 1 + n_dp - 1)
     v_left = halo_copy(vol.at[:, 0], halo_v.at[1], 0, left)
     v_right = halo_copy(vol.at[:, 3], halo_v.at[0], 1, right)
     v_left.start()
     v_right.start()
 
-    for z in range(4):
-        volume_layer(z + 1, vol[:, z].reshape(128, 128))
+    for pair in (0, 2):
+        volume_layers(
+            (pair + 1, pair + 2), [vol[:, pair + n].reshape(128, 128) for n in range(2)]
+        )
 
     for copy in loads[1:]:
         copy.wait()
@@ -245,24 +266,28 @@
 
     v_left.wait_recv()
     v_right.wait_recv()
+    planes = []
     for side, keep in ((0, has_left), (1, has_right)):
         plane = halo_v[side].reshape(128, 128).astype(F32)
-        volume_layer(5 * side, jnp.where(keep, plane, 0.0).astype(BF))
+        planes.append(jnp.where(keep, plane, 0.0).astype(BF))
+    volume_layers((0, 5), planes)
 
     def first_window(q):
         qz, qy, qx = q // 4, (q // 2) % 2, q % 2
         return ext[qx, 2 * qz : 2 * qz + 4, 2 * qy : 2 * qy + 4].reshape(256, LANES)
 
-    p_copies = []
-    for qz in range(2):
-        for qq in range(4):
-            q = 4 * qz + qq
-            act = dot(w1p[...], first_window(q)).reshape(8, 32, LANES) + b1c[None]
-            act1[q] = act
-            pooled[qz, qq] = (jnp.sum(leaky(act), axis=0) * 0.125).astype(BF)
-        copy = halo_copy(pooled.at[qz], halo_p.at[1 - qz], 2 + qz, right if qz else left)
-        copy.start()
-        p_copies.append(copy)
+    for qy in range(2):
+        for qz in range(2):
+            for qx in range(2):
+                q = 4 * qz + 2 * qy + qx
+                act = dot(w1p[...], first_window(q)).reshape(8, 32, LANES) + b1c[None]
+                act1[q] = act
+                pooled[qz, 2 * qy + qx] = (jnp.sum(leaky(act), axis=0) * 0.125).astype(BF)
+            rows = slice(2 * qy, 2 * qy + 2)
+            halo_copy(
+                pooled.at[qz, rows], halo_p.at[1 - qz, rows], 2 + qz, right if qz else left
+            ).start()
+    p_copies = [halo_copy(pooled.at[qz], halo_p.at[1 - qz], 2 + qz, left) for qz in range(2)]
 
     for qz in range(2):
         window_layer(win2, 1 + qz, lambda j, qz=qz: pooled[qz, j], 32, None)
@@ -277,11 +302,12 @@
     grad_top = cot[...].astype(F32) * 0.125
     top = jnp.zeros((64, LANES), F32)
     backs = [[None, None], [None, None]]
-    d_copies = []
     for pz in range(2):
         p_copies[1 - pz].wait_recv()
+    for pz in range(2):
         keep = has_right if pz else has_left
         window_layer(win2, 3 * pz, lambda j, pz=pz: halo_p[pz, j], 32, keep)
+    for pz in range(2):
         for py in range(2):
             at = 2 * pz
             act = acc[2 * pz + py] + dot(
@@ -291,8 +317,10 @@
                 one = act[64 * px : 64 * px + 64] + b2c
                 top = top + leaky(one)
                 delta2[pz, 2 * py + px] = (grad_top * slope(one)).astype(BF)
+    for pz in range(2):
         window_layer(win3, pz, lambda j, pz=pz: delta2[pz, j], 64, None)
-        for qy in range(2):
+    for qy in range(2):
+        for pz in range(2):
             three = dot(w2f[...], win3[pz, qy : qy + 3].reshape(768, LANES))
             for a in range(3):
                 qz, part = 1 + pz - a, three[64 * a : 64 * a + 64]
@@ -301,21 +329,18 @@
                     backs[qz][qy] = part if there is None else there + part
                 else:
                     give[pz, qy] = part.astype(BF)
-        copy = halo_copy(give.at[pz], halo_d.at[1 - pz], 4 + pz, right if pz else left)
-        copy.start()
-        d_copies.append(copy)
+            halo_copy(
+                give.at[pz, qy], halo_d.at[1 - pz, qy], 4 + pz, right if pz else left
+            ).start()
+    d_copies = [halo_copy(give.at[pz], halo_d.at[1 - pz], 4 + pz, left) for pz in range(2)]
     top_out[...] = (top * 0.125).astype(BF)
 
-    ones = jnp.ones((16, LANES), BF)
-    grad = None
-    sums = None
-    for pz in range(2):
-        for py in range(2):
-            there = delta2[pz, 2 * py : 2 * py + 2].reshape(128, LANES)
-            term = dot_nt(second_window(pz, py, 0, 3), there)
-            part = dot_nt(ones, there)
-            grad = term if grad is None else grad + term
-            sums = part if sums is None else sums + part
+    both = [(pz, py) for pz in range(2) for py in range(2)]
+    there = jnp.concatenate(
+        [delta2[pz, 2 * py : 2 * py + 2].reshape(128, LANES) for pz, py in both], axis=1
+    )
+    grad = dot_nt(jnp.concatenate([second_window(*b, 0, 3) for b in both], axis=1), there)
+    sums = dot_nt(jnp.ones((16, 4 * LANES), BF), there)
     low = lane_of((16, 128)) < 64
     per2 = -(-SLOTS // n_dp)
     for k in range(27):
@@ -328,80 +353,38 @@
     for extra in range(SLOTS, per2 * (-(-SLOTS // per2))):
         g2[extra // per2, extra % per2] = jnp.zeros((16, 128), F32)
 
-    def to_dp(j):
-        return {"dp": j}
-
-    def to_space(j):
-        return {"space": j}
-
-    def to_g(j):
-        return {"dp": half * n_g + j}
-
-    def to_h(j):
-        return {"dp": (j // n_sp) * n_g + g, "space": lax.rem(j, n_sp)}
-
-    def send_all(me, n, owners, where, src, dst, send, recv, start):
-        for r in range(1, n):
-            to = lax.rem(me + r, n)
+    def send_all(me, others, src, dst, sem, owners=None):
+        for to, device in others:
 
             def one():
-                copy = pltpu.make_async_remote_copy(
+                pltpu.make_async_remote_copy(
                     src_ref=src(to),
                     dst_ref=dst,
-                    send_sem=send.at[to],
-                    recv_sem=recv.at[me],
-                    device_id=where(to),
+                    send_sem=send_sem.at[sem],
+                    recv_sem=recv_sem.at[sem],
+                    device_id=device,
                     device_id_type=MESH,
-                )
-                if start:
-                    copy.start()
-                else:
-                    copy.wait_send()
-
-            if owners < n:
+                ).start()
+
+            if owners is None:
+                one()
+            else:
                 pl.when(to < owners)(one)
-            else:
-                one()
-
-    def take_all(me, n, owners, where, land, send, recv):
-        for r in range(1, n):
-            come = lax.rem(me + r, n)
-
-            def one():
-                pltpu.make_async_remote_copy(
-                    src_ref=land.at[come],
-                    dst_ref=land.at[come],
-                    send_sem=send.at[come],
-                    recv_sem=recv.at[come],
-                    device_id=where(come),
-                    device_id_type=MESH,
-                ).wait_recv()
-
-            if owners < n:
-                pl.when(come < owners)(one)
-            else:
-                one()
+
+    def all_of(ref, n, sem):
+        return pltpu.make_async_remote_copy(
+            src_ref=ref.at[0:n],
+            dst_ref=ref.at[0:n],
+            send_sem=send_sem.at[sem],
+            recv_sem=recv_sem.at[sem],
+            device_id={"space": right},
+            device_id_type=MESH,
+        )
 
     own2 = -(-SLOTS // per2)
     per1 = TILES // n_g
 
-    def start_a2(start):
-        send_all(d, n_dp, own2, to_dp, lambda to: g2.at[to], r2.at[d], send_a2, recv_a2, start)
-
-    def start_b2(start):
-        send_all(s, n_sp, n_sp, to_space, lambda to: s2.at[s], s2.at[s], send_b2, recv_b2, start)
-
-    def start_c2(start):
-        send_all(d, n_dp, n_dp, to_dp, lambda to: t2, f2.at[d], send_c2, recv_c2, start)
-
-    def start_a1(start):
-        send_all(g, n_g, n_g, to_g, lambda to: g1.at[to], r1.at[g], send_a1, recv_a1, start)
-
-    def start_b1(start):
-        send_all(h, n_h, n_h, to_h, lambda to: s1.at[h], s1.at[h], send_b1, recv_b1, start)
-
-    def start_c1(start):
-        send_all(g, n_g, n_g, to_g, lambda to: t1, f1.at[g], send_c1, recv_c1, start)
+    is_owner = d < own2
 
     def added(ref, n):
         total = ref[0]
@@ -409,81 +392,89 @@
             total = total + ref[j]
         return total
 
-    start_a2(True)
-
-    grad1 = None
-    sum1 = None
+    send_all(d, dp_peers, lambda to: g2.at[to], r2.at[d], 6, own2)
+
+    for q in range(8):
+        act1[q] = jnp.where(act1[q] > 0, 0.125, 0.3 * 0.125)
+
+    for qz in range(2):
+        d_copies[1 - qz].wait_recv()
     for qz in range(2):
         keep = has_right if qz else has_left
-        d_copies[1 - qz].wait_recv()
         for qy in range(2):
             back = backs[qz][qy] + jnp.where(keep, halo_d[qz, qy].astype(F32), 0.0)
-            back = back * 0.125
             for qx in range(2):
                 q = 4 * qz + 2 * qy + qx
                 one = back[32 * qx : 32 * qx + 32]
-                delta1 = (one[None] * slope(act1[q])).astype(BF).reshape(256, LANES)
-                term = dot_nt(delta1, first_window(q))
-                part = dot_nt(ones[0:16], delta1)
-                grad1 = term if grad1 is None else grad1 + term
-                sum1 = part if sum1 is None else sum1 + part
+                d1[:, LANES * q : LANES * q + LANES] = (
+                    (one[None] * act1[q]).astype(BF).reshape(256, LANES)
+                )
+    windows = jnp.concatenate([first_window(q) for q in range(8)], axis=1)
+    grad1 = dot_nt(d1[...], windows)
+    sum1 = dot_nt(d1[...], jnp.ones((128, 8 * LANES), BF))
     fold = grad1[0:32]
+    bias = sum1[0:32]
     for p in range(1, 8):
         by = 4 * (16 * (p // 4) + 4 * ((p // 2) % 2) + p % 2)
         fold = fold + pltpu.roll(grad1[32 * p : 32 * p + 32], LANES - by, 1)
-    bias = sum1[0:8, 0:128] + sum1[0:8, 128:256]
-    bias = bias + pltpu.roll(bias, 64, 1)
-    bias = bias + pltpu.roll(bias, 96, 1)
-    fold = jnp.where(lane_of((32, LANES)) == LANES - 1, column(bias[0:1, 0:32]), fold)
+        bias = bias + sum1[32 * p : 32 * p + 32]
+    fold = jnp.where(
+        lane_of((32, LANES)) == LANES - 1, jnp.concatenate([bias, bias], axis=1), fold
+    )
     for t in range(8):
         rt, lt = t // 2, t % 2
         g1[t // per1, t % per1] = fold[8 * rt : 8 * rt + 8, 128 * lt : 128 * lt + 128]
 
-    start_a1(True)
-
-    @pl.when(d < own2)
+    send_all(g, g_peers, lambda to: g1.at[to], r1.at[g], 7)
+
+    @pl.when(is_owner)
     def _():
         r2[d] = g2[d]
-        take_all(d, n_dp, n_dp, to_dp, r2, send_a2, recv_a2)
+        all_of(r2, n_dp - 1, 6).wait_recv()
         s2[s] = added(r2, n_dp)
-        start_b2(True)
+        send_all(s, s_peers, lambda to: s2.at[s], s2.at[s], 8)
 
     r1[g] = g1[g]
-    take_all(g, n_g, n_g, to_g, r1, send_a1, recv_a1)
+    all_of(r1, n_g - 1, 7).wait_recv()
     s1[h] = added(r1, n_g)
-    start_b1(True)
+    send_all(h, h_peers, lambda to: s1.at[h], s1.at[h], 9)
 
     mine2 = pltpu.make_async_copy(t2, f2.at[d], local_sem.at[0])
     mine1 = pltpu.make_async_copy(t1, f1.at[g], local_sem.at[1])
 
-    @pl.when(d < own2)
+    @pl.when(is_owner)
     def _():
-        take_all(s, n_sp, n_sp, to_space, s2, send_b2, recv_b2)
+        all_of(s2, n_sp - 1, 8).wait_recv()
         t2[...] = added(s2, n_sp).astype(BF)
-        start_c2(True)
+        send_all(d, dp_peers, lambda to: t2, f2.at[d], 10)
         mine2.start()
 
-    take_all(h, n_h, n_h, to_h, s1, send_b1, recv_b1)
+    all_of(s1, n_h - 1, 9).wait_recv()
     t1[...] = added(s1, n_h)
-    start_c1(True)
+    send_all(g, g_peers, lambda to: t1, f1.at[g], 11)
     mine1.start()
 
     for copy in [v_left, v_right] + p_copies + d_copies:
         copy.wait_send()
-    start_a2(False)
-    start_a1(False)
-    start_b1(False)
-
-    @pl.when(d < own2)
+    all_of(g1, n_g - 1, 7).wait_send()
+    all_of(s1, n_h - 1, 9).wait_send()
+
+    @pl.when(is_owner)
     def _():
-        start_b2(False)
+        all_of(g2, own2 - 1, 6).wait_send()
+        all_of(s2, n_sp - 1, 8).wait_send()
         mine2.wait()
-        start_c2(False)
+        all_of(f2, n_dp - 1, 10).wait_send()
+        all_of(f2, own2 - 1, 10).wait_recv()
+
+    @pl.when(jnp.logical_not(is_owner))
+    def _():
+        all_of(g2, own2, 6).wait_send()
+        all_of(f2, own2, 10).wait_recv()
 
     mine1.wait()
-    start_c1(False)
-    take_all(d, n_dp, own2, to_dp, f2, send_c2, recv_c2)
-    take_all(g, n_g, n_g, to_g, f1, send_c1, recv_c1)
+    all_of(f1, n_g - 1, 11).wait_send()
+    all_of(f1, n_g - 1, 11).wait_recv()
 
 
 def finish(per2, per1, top, f1, f2, top_out, gw1_out, gb1_out, gw2_out, gb2_out):
@@ -507,7 +498,6 @@
 def solution(mesh):
     n_dp, n_sp = mesh.shape["dp"], mesh.shape["space"]
     per2 = -(-SLOTS // n_dp)
-    own2 = -(-SLOTS // per2)
     n_g, n_h = n_dp // 2, 2 * n_sp
     per1 = TILES // n_g
     vm = pl.BlockSpec(memory_space=pltpu.VMEM)
@@ -519,7 +509,7 @@
             out_shape=(
                 jax.ShapeDtypeStruct((64, LANES), BF),
                 jax.ShapeDtypeStruct((n_g, per1, 8, 128), F32),
-                jax.ShapeDtypeStruct((own2, per2, 16, 128), BF),
+                jax.ShapeDtypeStruct((n_dp, per2, 16, 128), BF),
             ),
             in_specs=[anywhere] * 6,
             out_specs=(vm, anywhere, anywhere),
@@ -546,6 +536,7 @@
                 pltpu.VMEM((2, 2, 64, LANES), BF),
                 pltpu.VMEM((2, 4, 256, LANES), BF),
                 pltpu.VMEM((4, 128, LANES), F32),
+                pltpu.VMEM((256, 8 * LANES), BF),
                 pltpu.VMEM((n_dp, per2, 16, 128), F32),
                 pltpu.VMEM((n_dp, per2, 16, 128), F32),
                 pltpu.VMEM((n_sp, per2, 16, 128), F32),
@@ -555,12 +546,7 @@
                 pltpu.VMEM((n_h, per1, 8, 128), F32),
                 pltpu.VMEM((per1, 8, 128), F32),
             ]
-            + [
-                pltpu.SemaphoreType.DMA((n,))
-                for n in (6, 6, 6)
-                + (n_dp, n_dp, n_sp, n_sp, n_dp, n_dp)
-                + (n_g, n_g, n_h, n_h, n_g, n_g)
-            ],
+            + [pltpu.SemaphoreType.DMA((n,)) for n in (6, 12, 12)],
             compiler_params=pltpu.CompilerParams(collective_id=0, has_side_effects=True),
             name="step",
         )(

time: 43.1 us -> 41.9 us (0.972)
  Pallas kernels: 42.4 us -> 41.1 us
    pallas_call x1, Pallas kernels: 40.5 us -> 39.3 us  [body(): pl.pallas_call(functools.partial(kernel, n_dp, n_sp), out_shape=(jax.Shap...]
where the time goes in v2:
time: 41.9 us; the launch traced here: 41.8 us
  Pallas kernels  41.1 us (98%)
  between operations  0.64 us (2%)
    pallas_call x1, Pallas kernels, body(): pl.pallas_call(functools.partial(kernel, n_dp, n_sp), out_shape=(jax.Shap...  39.3 us
    pallas_call x1, Pallas kernels, body(): pl.pallas_call(functools.partial(finish, per2, per1), out_shape=(jax.Shap...  1.82 us

profile of v2, /device:TPU:1, one launch (start us, length us, event | category | flops | bytes accessed | tf_op | source)
XLA Modules:
  0.0 41.8 jit_solution(3320203313843946951)
XLA Ops:
  0.6 39.3 %step.1 = (bf16[64,256]{1,0:T(8,128)(2,1)}, f32[8,1,8,128]{3,2,1,0:T(8,128)}, bf16[16,2,16,128]{3,2,1,0:T(8,128)(2,1)}) custom-call(bf16[4,4,32,128]{3,2,1,0:T(8,128)(2,1)} %bitcast.12, bf16[27,4,32]{2,1,0:T(4,128)(2,1)} %bitcast.14, f32[1,32]{1,0:T(1,128)} %bitcast.15, bf16[27,32,64]{2,1,0:T(8,128)(2,1)} %bitcast.11, f32[1,64]{1,0:T(1,128)} %bitcast.16, ...), custom_call_target="tpu_custom_call" | custom-call | tf_op jit(solution)/shard_map/step/pallas_call | solution.py:507
  39.9 1.8 %finish.1 = (bf16[64,256]{1,0:T(8,128)(2,1)}, f32[27,4,32]{2,1,0:T(4,128)}, f32[1,32]{1,0:T(1,128)}, f32[27,32,64]{2,1,0:T(8,128)}, f32[1,64]{1,0:T(1,128)}) custom-call(bf16[64,256]{1,0:T(8,128)(2,1)} %get-tuple-element.13.top, f32[8,1,8,128]{3,2,1,0:T(8,128)} %get-tuple-element.14.f1, bf16[16,2,16,128]{3,2,1,0:T(8,128)(2,1)} %get-tuple-element.15.f2), custom_call_target="tpu_custom_call" | custom-call | tf_op jit(solution)/shard_map/finish/pallas_call | solution.py:560

commit v3 on v2

--- a/solution.py
+++ b/solution.py
@@ -92,6 +92,7 @@
     b2,
     cot,
     pick,
+    edge_v,
     halo_v,
     ext,
     base_w,
@@ -184,10 +185,10 @@
     for copy in loads:
         copy.start()
 
-    for f in range(6):
+    for f in range(4):
         r = lax.broadcasted_iota(jnp.int32, (128, LANES), 0)
         c = lane_of((128, LANES)) % COLS
-        pick[:, f * LANES : (f + 1) * LANES] = jnp.where(r == 4 * c + f - 1, 1.0, 0.0).astype(BF)
+        pick[:, f * LANES : (f + 1) * LANES] = jnp.where(r == 4 * c + f, 1.0, 0.0).astype(BF)
     row = lax.broadcasted_iota(jnp.int32, (64, 512), 0)
     col = lax.broadcasted_iota(jnp.int32, (64, 512), 1)
     gather = jnp.where(
@@ -199,20 +200,29 @@
         (256, LANES)
     ) // COLS
 
-    def volume_layers(layers, planes):
+    def split(planes):
         both = jnp.concatenate(planes, axis=0)
         parts = []
-        for f in range(6):
+        for f in range(4):
             spread = dot(both, pick[:, f * LANES : (f + 1) * LANES])
             parts.append(jnp.where(own_y, spread, 0.0).astype(BF))
-        for n, layer in enumerate(layers):
-            for qx in range(2):
-                mine = [part[128 * n : 128 * n + 128] for part in parts[2 * qx : 2 * qx + 4]]
-                cells = dot(gather, jnp.concatenate(mine, axis=0))
-                ext[qx, layer, 0] = shift_y(cells[48:64], 1).astype(BF)
-                for fy in range(4):
-                    ext[qx, layer, fy + 1] = cells[16 * fy : 16 * fy + 16].astype(BF)
-                ext[qx, layer, 5] = shift_y(cells[0:16], -1).astype(BF)
+        return [
+            dot(gather, jnp.concatenate([part[128 * n : 128 * n + 128] for part in parts], axis=0))
+            for n in range(2)
+        ]
+
+    def first_layer(layer, cells):
+        at = lax.broadcasted_iota(jnp.int32, (64, LANES), 0) % 16
+        before = pltpu.roll(shift_x(cells, 1), 64 - 12, 0)
+        after = pltpu.roll(shift_x(cells, -1), 12, 0)
+        wide = (
+            jnp.where(at >= 4, pltpu.roll(cells, 4, 0), before),
+            jnp.where(at < 12, pltpu.roll(cells, 64 - 4, 0), after),
+        )
+        for qx in range(2):
+            ext[qx, layer, 0] = shift_y(wide[qx][48:64], 1).astype(BF)
+            ext[qx, layer, 1:5] = wide[qx].astype(BF).reshape(4, 16, LANES)
+            ext[qx, layer, 5] = shift_y(wide[qx][0:16], -1).astype(BF)
 
     def halo_copy(src, dst, sem, to):
         return pltpu.make_async_remote_copy(
@@ -225,16 +235,12 @@
         )
 
     loads[0].wait()
-    pl.semaphore_wait(barrier, n_h - 1 + n_dp - 1)
-    v_left = halo_copy(vol.at[:, 0], halo_v.at[1], 0, left)
-    v_right = halo_copy(vol.at[:, 3], halo_v.at[0], 1, right)
-    v_left.start()
-    v_right.start()
-
-    for pair in (0, 2):
-        volume_layers(
-            (pair + 1, pair + 2), [vol[:, pair + n].reshape(128, 128) for n in range(2)]
-        )
+    for pair in ((0, 3), (1, 2)):
+        cells = split([vol[:, z].reshape(128, 128) for z in pair])
+        for n, z in enumerate(pair):
+            if pair == (0, 3):
+                edge_v[n] = cells[n].astype(BF)
+            first_layer(z + 1, cells[n])
 
     for copy in loads[1:]:
         copy.wait()
@@ -264,13 +270,15 @@
     b1c = column(b1[...])
     b2c = column(b2[...])
 
+    pl.semaphore_wait(barrier, n_h - 1 + n_dp - 1)
+    v_left = halo_copy(edge_v.at[0], halo_v.at[1], 0, left)
+    v_right = halo_copy(edge_v.at[1], halo_v.at[0], 1, right)
+    v_left.start()
+    v_right.start()
     v_left.wait_recv()
     v_right.wait_recv()
-    planes = []
     for side, keep in ((0, has_left), (1, has_right)):
-        plane = halo_v[side].reshape(128, 128).astype(F32)
-        planes.append(jnp.where(keep, plane, 0.0).astype(BF))
-    volume_layers((0, 5), planes)
+        first_layer(5 * side, jnp.where(keep, halo_v[side].astype(F32), 0.0))
 
     def first_window(q):
         qz, qy, qx = q // 4, (q // 2) % 2, q % 2
@@ -283,7 +291,8 @@
                 act = dot(w1p[...], first_window(q)).reshape(8, 32, LANES) + b1c[None]
                 act1[q] = act
                 pooled[qz, 2 * qy + qx] = (jnp.sum(leaky(act), axis=0) * 0.125).astype(BF)
-            rows = slice(2 * qy, 2 * qy + 2)
+        rows = slice(2 * qy, 2 * qy + 2)
+        for qz in range(2):
             halo_copy(
                 pooled.at[qz, rows], halo_p.at[1 - qz, rows], 2 + qz, right if qz else left
             ).start()
@@ -339,16 +348,19 @@
     there = jnp.concatenate(
         [delta2[pz, 2 * py : 2 * py + 2].reshape(128, LANES) for pz, py in both], axis=1
     )
-    grad = dot_nt(jnp.concatenate([second_window(*b, 0, 3) for b in both], axis=1), there)
     sums = dot_nt(jnp.ones((16, 4 * LANES), BF), there)
     low = lane_of((16, 128)) < 64
     per2 = -(-SLOTS // n_dp)
-    for k in range(27):
-        at = 128 * (k // 3) + 32 * (k % 3)
-        here, after = grad[at : at + 32], grad[at + 32 : at + 64]
-        first = here[0:16] + pltpu.roll(after[0:16], 64, 1)
-        second = pltpu.roll(here[16:32], 64, 1) + after[16:32]
-        g2[k // per2, k % per2] = jnp.where(low, first, second)
+    for a in range(3):
+        grad = dot_nt(
+            jnp.concatenate([second_window(*b, a, a + 1) for b in both], axis=1), there
+        )
+        for n in range(9):
+            k, at = 9 * a + n, 128 * (n // 3) + 32 * (n % 3)
+            here, after = grad[at : at + 32], grad[at + 32 : at + 64]
+            first = here[0:16] + pltpu.roll(after[0:16], 64, 1)
+            second = pltpu.roll(here[16:32], 64, 1) + after[16:32]
+            g2[k // per2, k % per2] = jnp.where(low, first, second)
     g2[27 // per2, 27 % per2] = sums + pltpu.roll(sums, 64, 1)
     for extra in range(SLOTS, per2 * (-(-SLOTS // per2))):
         g2[extra // per2, extra % per2] = jnp.zeros((16, 128), F32)
@@ -399,28 +411,26 @@
 
     for qz in range(2):
         d_copies[1 - qz].wait_recv()
+    grad1 = None
+    bias = jnp.zeros((32, LANES), F32)
     for qz in range(2):
         keep = has_right if qz else has_left
         for qy in range(2):
             back = backs[qz][qy] + jnp.where(keep, halo_d[qz, qy].astype(F32), 0.0)
             for qx in range(2):
                 q = 4 * qz + 2 * qy + qx
-                one = back[32 * qx : 32 * qx + 32]
-                d1[:, LANES * q : LANES * q + LANES] = (
-                    (one[None] * act1[q]).astype(BF).reshape(256, LANES)
-                )
-    windows = jnp.concatenate([first_window(q) for q in range(8)], axis=1)
-    grad1 = dot_nt(d1[...], windows)
-    sum1 = dot_nt(d1[...], jnp.ones((128, 8 * LANES), BF))
+                one = (back[32 * qx : 32 * qx + 32][None] * act1[q]).astype(BF)
+                bias = bias + jnp.sum(one.astype(F32), axis=0)
+                d1[:, LANES * q : LANES * q + LANES] = one.reshape(256, LANES)
+        windows = jnp.concatenate([first_window(4 * qz + j) for j in range(4)], axis=1)
+        term = dot_nt(d1[:, 4 * LANES * qz : 4 * LANES * (qz + 1)], windows)
+        grad1 = term if grad1 is None else grad1 + term
     fold = grad1[0:32]
-    bias = sum1[0:32]
     for p in range(1, 8):
         by = 4 * (16 * (p // 4) + 4 * ((p // 2) % 2) + p % 2)
         fold = fold + pltpu.roll(grad1[32 * p : 32 * p + 32], LANES - by, 1)
-        bias = bias + sum1[32 * p : 32 * p + 32]
-    fold = jnp.where(
-        lane_of((32, LANES)) == LANES - 1, jnp.concatenate([bias, bias], axis=1), fold
-    )
+    bias = jnp.broadcast_to(jnp.sum(bias, axis=1, keepdims=True), (32, LANES))
+    fold = jnp.where(lane_of((32, LANES)) == LANES - 1, bias, fold)
     for t in range(8):
         rt, lt = t // 2, t % 2
         g1[t // per1, t % per1] = fold[8 * rt : 8 * rt + 8, 128 * lt : 128 * lt + 128]
@@ -520,8 +530,9 @@
                 pltpu.VMEM((27, 32, 64), BF),
                 pltpu.VMEM((1, 64), F32),
                 pltpu.VMEM((64, LANES), BF),
-                pltpu.VMEM((128, 6 * LANES), BF),
-                pltpu.VMEM((2, 4, 32, 128), BF),
+                pltpu.VMEM((128, 4 * LANES), BF),
+                pltpu.VMEM((2, 64, LANES), BF),
+                pltpu.VMEM((2, 64, LANES), BF),
                 pltpu.VMEM((2, 6, 6, 16, LANES), BF),
                 pltpu.VMEM((256, 128), F32),
                 pltpu.VMEM((256, 256), BF),

time: 41.9 us -> 41 us (0.979)
  Pallas kernels: 41.1 us -> 40.2 us
    pallas_call x1, Pallas kernels: 39.3 us -> 38.3 us  [body(): pl.pallas_call(functools.partial(kernel, n_dp, n_sp), out_shape=(jax.Shap...]
where the time goes in v3:
time: 41 us; the launch traced here: 40.8 us
  Pallas kernels  40.2 us (98%)
  between operations  0.64 us (2%)
    pallas_call x1, Pallas kernels, body(): pl.pallas_call(functools.partial(kernel, n_dp, n_sp), out_shape=(jax.Shap...  38.3 us
    pallas_call x1, Pallas kernels, body(): pl.pallas_call(functools.partial(finish, per2, per1), out_shape=(jax.Shap...  1.82 us

profile of v3, /device:TPU:1, one launch (start us, length us, event | category | flops | bytes accessed | tf_op | source)
XLA Modules:
  0.0 40.8 jit_solution(8462992478028435368)
XLA Ops:
  0.6 38.3 %step.1 = (bf16[64,256]{1,0:T(8,128)(2,1)}, f32[8,1,8,128]{3,2,1,0:T(8,128)}, bf16[16,2,16,128]{3,2,1,0:T(8,128)(2,1)}) custom-call(bf16[4,4,32,128]{3,2,1,0:T(8,128)(2,1)} %bitcast.12, bf16[27,4,32]{2,1,0:T(4,128)(2,1)} %bitcast.14, f32[1,32]{1,0:T(1,128)} %bitcast.15, bf16[27,32,64]{2,1,0:T(8,128)(2,1)} %bitcast.11, f32[1,64]{1,0:T(1,128)} %bitcast.16, ...), custom_call_target="tpu_custom_call" | custom-call | tf_op jit(solution)/shard_map/step/pallas_call | solution.py:517
  39.0 1.8 %finish.1 = (bf16[64,256]{1,0:T(8,128)(2,1)}, f32[27,4,32]{2,1,0:T(4,128)}, f32[1,32]{1,0:T(1,128)}, f32[27,32,64]{2,1,0:T(8,128)}, f32[1,64]{1,0:T(1,128)}) custom-call(bf16[64,256]{1,0:T(8,128)(2,1)} %get-tuple-element.13.top, f32[8,1,8,128]{3,2,1,0:T(8,128)} %get-tuple-element.14.f1, bf16[16,2,16,128]{3,2,1,0:T(8,128)(2,1)} %get-tuple-element.15.f2), custom_call_target="tpu_custom_call" | custom-call | tf_op jit(solution)/shard_map/finish/pallas_call | solution.py:571
